TPU v7x, 256 devices: a whole 4x4x8 slice. The times are simulated.
256 devices in a mesh: energy: 16 (over z, core), cell: 16 (over y, x).
Axes of the slice: x: 4, y: 4, z: 8, core: 2. Of those that a mesh axis runs over, the one named last changes fastest.
Arguments:
- green: bfloat16 [4, 96, 32, 16, 512], P(None, 'energy', 'cell'), may hold values from -6 to 6
- screened: bfloat16 [4, 96, 32, 16, 512], P(None, 'energy', None, 'cell'), may hold values from -6 to 6
- cell_map: int32 [32], replicated, may hold values from 0 to 31, each once
- shift_table: int32 [16, 16, 3], replicated, may hold values from 0 to 5, as said below
- shift_count: int32 [16, 16], replicated, may hold values from 1 to 3, as said below
Outputs:
- sigma: float32 [4, 96, 32, 16, 512], P(None, 'energy', 'cell')
Inputs may be any that keep to these rules, and one draw needn't show every extreme that they name: `shift_table`: offsets of requested energies within the source group; slots c >= shift_count[g, s] are not read. `shift_count`: some destination group requests 3 energies from every source group. `cell_map`: each cell stands at exactly one position.
All inputs are finite; a program needn't handle non-finite values.
Results may differ from a plain program's by a relative error of at most 0.0003.
Values may be sent and summed in bfloat16 or wider, within the bound.
A program may use at most 128 MiB of HBM per device.

v0:
```python
import jax
import jax.numpy as jnp
from jax import lax
from jax.sharding import PartitionSpec as P

SCALE = 0.2


def per_device(green, screened, cell_map, shift_table, shift_count):
    groups = lax.axis_size("energy")
    cell_count = lax.axis_size("cell")
    per_energy = green.shape[1]
    per_cell = green.shape[2]
    width = green.shape[4]
    slot_count = shift_table.shape[2]
    wanted = jnp.transpose(cell_map.reshape(cell_count, per_cell)).reshape(-1)
    outgoing = jnp.take(screened, wanted, axis=2)
    outgoing = outgoing.reshape(4, per_energy, per_cell, cell_count, screened.shape[3], width)
    arrived = lax.all_to_all(outgoing, "cell", split_axis=3, concat_axis=3, tiled=True)
    owned = arrived.reshape(4, per_energy, per_cell, green.shape[3], width)
    whole = lax.all_gather(green, "energy", axis=1, tiled=True)
    padding = jnp.zeros((4, per_energy) + whole.shape[2:], whole.dtype)
    padded = jnp.concatenate([padding, whole], axis=1)
    group = lax.axis_index("energy")
    first = group * per_energy
    table_row = shift_table[group]
    counts = shift_count[group]
    every = lax.all_gather(owned, "energy", axis=1, tiled=True)

    def values_of(energy):
        return lax.dynamic_index_in_dim(every, energy, 1, keepdims=False)

    def turn(totals, source):
        sums = list(totals)
        for slot in range(slot_count):
            energy = source * per_energy + table_row[source, slot]
            live = (slot < counts[source]).astype(jnp.float32)
            start = jnp.maximum(first - energy, -per_energy) + per_energy
            window = lax.dynamic_slice_in_dim(padded, start, per_energy, 1)
            value = values_of(energy)
            for kind in range(2):
                g_real = window[2 * kind].astype(jnp.float32)
                g_imag = window[2 * kind + 1].astype(jnp.float32)
                w_real = value[2 * kind].astype(jnp.float32)[None] * live
                w_imag = value[2 * kind + 1].astype(jnp.float32)[None] * live
                sums[2 * kind] = sums[2 * kind] - (g_real * w_imag + g_imag * w_real)
                sums[2 * kind + 1] = sums[2 * kind + 1] + (g_real * w_real - g_imag * w_imag)
        return (tuple(sums), None)

    zeros = jnp.zeros(green.shape[1:], jnp.float32)
    totals, _ = lax.scan(turn, (zeros, zeros, zeros, zeros), jnp.arange(groups, dtype=jnp.int32))
    return jnp.stack(totals, axis=0) * SCALE


def solution(mesh):
    placed = (
        P(None, "energy", "cell", None, None),
        P(None, "energy", None, "cell", None),
        P(),
        P(),
        P(),
    )
    return jax.shard_map(
        per_device,
        mesh=mesh,
        in_specs=placed,
        out_specs=P(None, "energy", "cell", None, None),
        check_vma=False,
    )
```

profile of v0, /device:TPU:1, one launch (start us, length us, event | category | flops | bytes accessed | tf_op | source)
XLA Modules:
  0.0 408.6 jit_solution(6469236370796020394)
XLA Ops:
  12.3 21.0 %all_to_all.5 = bf16[4,6,2,16,1,512]{5,2,1,0,4,3:T(2,128)(2,1)} all-to-all(bf16[4,6,2,16,1,512]{5,2,1,0,4,3:T(2,128)(2,1)S(1)} %broadcast_select_fusion), channel_id=1, replica_groups=mesh['energy'=16,'cell'=16] {'cell'}, dimensions={3} | all-to-all | bytes 1572864 | tf_op jit(solution)/shard_map/all_to_all | solution.py:19
  34.1 55.1 %all-gather.4.cloned.1.call-done = bf16[4,96,2,16,512]{4,3,2,1,0:T(8,128)(2,1)} async-done(((bf16[4,6,2,16,512]{4,3,2,1,0:T(8,128)(2,1)}), bf16[4,96,2,16,512]{4,3,2,1,0:T(8,128)(2,1)}) %all-gather.4.cloned.1.call-update) | async-done | bytes 12582928 | tf_op jit(solution)/shard_map/all_gather | solution.py:21
  89.1 11.3 %concatenate.3 = bf16[4,102,2,16,512]{4,3,2,1,0:T(8,128)(2,1)} pad(bf16[4,96,2,16,512]{4,3,2,1,0:T(8,128)(2,1)} %all-gather.4.cloned.1.call-done, bf16[]{:T(256)} %constant.96.clone.1), padding=0_0x6_0x0_0x0_0x0_0 | pad | bytes 25952258 | tf_op jit(solution)/shard_map/concatenate | solution.py:23
  100.5 64.7 %all-gather.6.cloned.1.call-done = bf16[4,96,2,16,1,512]{5,2,1,0,4,3:T(2,128)(2,1)} async-done(((bf16[4,6,2,16,1,512]{5,2,1,0,4,3:T(2,128)(2,1)}), bf16[4,96,2,16,1,512]{5,2,1,0,4,3:T(2,128)(2,1)}) %all-gather.6.cloned.1.call-update) | async-done | bytes 12582928 | tf_op jit(solution)/shard_map/all_gather | solution.py:28
  165.2 23.7 %copy.15 = bf16[4,96,2,16,512]{4,3,2,1,0:T(8,128)(2,1)} copy(bf16[4,96,2,16,512]{4,2,1,0,3:T(2,128)(2,1)} %bitcast.179) | data formatting | bytes 25165824
  188.9 211.5 %while.20 = (s32[]{:T(128)}, f32[6,2,16,512]{3,2,1,0:T(8,128)S(1)}, f32[6,2,16,512]{3,2,1,0:T(8,128)S(1)}, f32[6,2,16,512]{3,2,1,0:T(8,128)S(1)}, f32[6,2,16,512...) while((s32[]{:T(128)}, f32[6,2,16,512]{3,2,1,0:T(8,128)S(1)}, ...), condition=%wide.region_1.2_spmd.clone, body=%wide.region_0.1_spmd.clone.sunk | while | flops 6684718 | bytes 7471924 | solution.py:51
  198.6 1.8 fusion.28
  200.4 1.8 fusion.27
  211.8 1.8 fusion.28
  213.6 1.8 fusion.27
  225.0 1.8 fusion.28
  226.8 1.8 fusion.27
  238.2 1.8 fusion.28
  240.0 1.8 fusion.27
  251.4 1.8 fusion.28
  253.2 1.8 fusion.27
  264.7 1.8 fusion.28
  266.4 1.8 fusion.27
  277.9 1.8 fusion.28
  279.7 1.8 fusion.27
  291.1 1.8 fusion.28
  304.3 1.8 fusion.28
  306.1 1.8 fusion.27
  317.5 1.8 fusion.28
  319.3 1.8 fusion.27
  330.7 1.8 fusion.28
  344.0 1.8 fusion.28
  357.2 1.8 fusion.28
  359.0 1.8 fusion.27
  370.4 1.8 fusion.28
  383.6 1.8 fusion.28
  396.8 1.8 fusion.28
  (94 shorter events, 66.8 us)
Async XLA Ops:
  6.5 26.8 %copy-start = (s32[16,16,3]{1,0,2:T(8,128)S(1)}, s32[16,16,3]{1,0,2:T(8,128)}, u32[]{:S(2)}) copy-start(s32[16,16,3]{1,0,2:T(8,128)} %param.10) | copy-start | bytes 9220
  6.5 82.6 %all-gather.4.cloned.1.call-start = ((), (), s32[]{:S(2)}) async-start(), calls=%async_computation.1 | async-start | bytes 13369344 | tf_op jit(solution)/shard_map/all_gather | solution.py:21
  7.3 157.9 %all-gather.6.cloned.1.call-start = ((), (), s32[]{:S(2)}) async-start(), calls=%async_computation.2 | async-start | bytes 13369344 | tf_op jit(solution)/shard_map/all_gather | solution.py:28
Sparse Core Ops, SparseCore 0:
  9.2 79.8 all-gather.3
  91.0 74.1 all-gather.5
where the time goes:
time: 413 us; the launch traced here: 409 us
  waiting for transfers between devices  121 us (29%)
  loops' own time  106 us (26%)
  other arithmetic  76.4 us (18%)
  local copies, waits for them, and re-layouts  71.2 us (17%)
  blocking collectives  21 us (5%)
  between operations  13.5 us (3%)
    another operation x1, loops' own time, per_device(): lax.scan(turn, (zeros, zeros, zeros, zeros), jnp.arange(groups, dtype=jnp...  106 us
    all_gather x1, waiting for transfers between devices, per_device(): every = lax.all_gather(owned, 'energy', axis=1, tiled=True)  64.7 us
    add x32, other arithmetic, turn(): sums[2 * kind + 1] + (g_real * w_real - g_imag * w_imag)  57.2 us
    all_gather x1, waiting for transfers between devices, per_device(): whole = lax.all_gather(green, 'energy', axis=1, tiled=True)  55.1 us
    unnamed x5, local copies, waits for them, and re-layouts  25.5 us
    all_to_all x1, blocking collectives, per_device(): lax.all_to_all(outgoing, 'cell', split_axis=3, concat_axis=3, tiled=True)  21 us
    mul x16, other arithmetic, turn(): w_imag = value[2 * kind + 1].astype(jnp.float32)[None] * live  16.8 us
    concatenate x1, local copies, waits for them, and re-layouts, per_device(): padded = jnp.concatenate([padding, whole], axis=1)  11.3 us
  transfers between devices with their start and end apart: 2, of which 2 were waited for; matrix products, arithmetic and copies ran while one was open for 4% of the time, Pallas kernels for 0%

commit v1 on v0

--- a/solution.py
+++ b/solution.py
@@ -16,7 +16,18 @@
     wanted = jnp.transpose(cell_map.reshape(cell_count, per_cell)).reshape(-1)
     outgoing = jnp.take(screened, wanted, axis=2)
     outgoing = outgoing.reshape(4, per_energy, per_cell, cell_count, screened.shape[3], width)
-    arrived = lax.all_to_all(outgoing, "cell", split_axis=3, concat_axis=3, tiled=True)
+    known, value_now = (lax.axis_size("cell"), lax.axis_index("cell"))
+    z2 = outgoing.shape[3] // known
+    y = list(outgoing.shape)
+    y[3] = z2
+    s_next = y[3]
+    y[3] = s_next * known
+    arrived = jnp.zeros(y, outgoing.dtype)
+    for d in range(known):
+        then = lax.dynamic_slice_in_dim(outgoing, (value_now ^ d) * z2, z2, axis=3)
+        if d:
+            then = lax.ppermute(then, "cell", tuple(((h, h ^ d) for h in range(known))))
+        arrived = lax.dynamic_update_slice_in_dim(arrived, then, (value_now ^ d) * s_next, axis=3)
     owned = arrived.reshape(4, per_energy, per_cell, green.shape[3], width)
     whole = lax.all_gather(green, "energy", axis=1, tiled=True)
     padding = jnp.zeros((4, per_energy) + whole.shape[2:], whole.dtype)

time: 413 us -> 387 us (0.937)
  starting transfers between devices: 0.04 us -> 29.3 us
  waiting for transfers between devices: 121 us -> 95.3 us
  blocking collectives: 21 us -> 0 us
  local copies, waits for them, and re-layouts: 71.2 us -> 62.8 us
    all_gather x1, waiting for transfers between devices: 55.1 us -> 22.6 us  [per_device(): whole = lax.all_gather(green, 'energy', axis=1, tiled=True)]
    ppermute x0 -> x15, starting transfers between devices: none -> 29.3 us  [per_device(): then = lax.ppermute(then, 'cell', tuple(((h, h ^ d) for h in range(known))))]
    unnamed x5 -> x6, local copies, waits for them, and re-layouts: 25.5 us -> 2.64 us
    all_to_all x1 -> x0, blocking collectives: 21 us -> none  [per_device(): lax.all_to_all(outgoing, 'cell', split_axis=3, concat_axis=3, tiled=True)]
    dynamic_update_slice x0 -> x16, local copies, waits for them, and re-layouts: none -> 13.8 us  [per_device(): lax.dynamic_update_slice_in_dim(arrived, then, (value_now ^ d) * s_next,...]
    ppermute x0 -> x15, waiting for transfers between devices: none -> 7.29 us  [per_device(): then = lax.ppermute(then, 'cell', tuple(((h, h ^ d) for h in range(known))))]
  transfers between devices with their start and end apart: 2 -> 17, of which waited for: 2 -> 3; matrix products, arithmetic and copies ran while one was open for 4% -> 9% of each run, Pallas kernels for 0% -> 0%
where the time goes in v1:
time: 387 us; the launch traced here: 383 us
  loops' own time  105 us (27%)
  waiting for transfers between devices  95.3 us (25%)
  other arithmetic  76.1 us (20%)
  local copies, waits for them, and re-layouts  62.8 us (16%)
  starting transfers between devices  29.3 us (8%)
  between operations  13.9 us (4%)
    another operation x1, loops' own time, per_device(): lax.scan(turn, (zeros, zeros, zeros, zeros), jnp.arange(groups, dtype=jnp...  105 us
    all_gather x1, waiting for transfers between devices, per_device(): every = lax.all_gather(owned, 'energy', axis=1, tiled=True)  64.7 us
    add x32, other arithmetic, turn(): sums[2 * kind + 1] + (g_real * w_real - g_imag * w_imag)  57.8 us
    ppermute x15, starting transfers between devices, per_device(): then = lax.ppermute(then, 'cell', tuple(((h, h ^ d) for h in range(known))))  29.3 us
    all_gather x1, waiting for transfers between devices, per_device(): whole = lax.all_gather(green, 'energy', axis=1, tiled=True)  22.6 us
    mul x16, other arithmetic, turn(): w_imag = value[2 * kind + 1].astype(jnp.float32)[None] * live  16.9 us
    dynamic_update_slice x16, local copies, waits for them, and re-layouts, per_device(): lax.dynamic_update_slice_in_dim(arrived, then, (value_now ^ d) * s_next,...  13.8 us
    concatenate x1, local copies, waits for them, and re-layouts, per_device(): padded = jnp.concatenate([padding, whole], axis=1)  11.4 us
  transfers between devices with their start and end apart: 17, of which 3 were waited for; matrix products, arithmetic and copies ran while one was open for 9% of the time, Pallas kernels for 0%

profile of v1, /device:TPU:1, one launch (start us, length us, event | category | flops | bytes accessed | tf_op | source)
XLA Modules:
  0.0 382.7 jit_solution(8435021029583829166)
XLA Ops:
  11.9 2.3 constant_dynamic-slice_fusion.4
  14.2 6.3 %collective-permute-start.9 = (bf16[4,6,2,1,1,512]{5,3,2,1,0,4:T(2,128)(2,1)S(1)}, bf16[4,6,2,1,1,512]{5,3,2,1,0,4:T(2,128)(2,1)S(1)}, u32[]{:S(2)}, u32[]{:S(2)}) collective-permute-start(bf16[4,6,2,1,1,512]{5,3,2,1,0,4:T(2,128)(2,1)S(1)} %get-tuple-element.260), channel_id=1, source_target_pairs={{0,10},{1,11},{2,8},{3,9},{4,14},{5,15},{6,12},{7,13},{8,2},{9,3},... | collective-permute-start | bytes 147464 | tf_op jit(solution)/shard_map/ppermute | solution.py:29
  20.6 2.9 collective-permute-start.7
  23.8 3.5 collective-permute-start.5
  28.9 7.3 %collective-permute-done.7 = bf16[4,6,2,1,1,512]{5,3,2,1,0,4:T(2,128)(2,1)S(1)} collective-permute-done((bf16[4,6,2,1,1,512]{5,3,2,1,0,4:T(2,128)(2,1)S(1)}, bf16[4,6,2,1,1,512]{5,3,2,1,0,4:T(2,128)(2,1)S(1)}, u32[]{:S(2)}, u32[]{:S(2)}) %collective-permute-start.7) | collective-permute-done | bytes 49184 | tf_op jit(solution)/shard_map/ppermute | solution.py:29
  39.4 3.1 collective-permute-start.10
  45.1 2.5 collective-permute-start.13
  47.6 3.2 collective-permute-start.14
  66.5 22.6 %all-gather.3.cloned.1.call-done = bf16[4,96,2,16,512]{4,3,2,1,0:T(8,128)(2,1)} async-done(((bf16[4,6,2,16,512]{4,3,2,1,0:T(8,128)(2,1)}), bf16[4,96,2,16,512]{4,3,2,1,0:T(8,128)(2,1)}) %all-gather.3.cloned.1.call-update) | async-done | bytes 12582928 | tf_op jit(solution)/shard_map/all_gather | solution.py:32
  89.1 11.4 %concatenate.3 = bf16[4,102,2,16,512]{4,3,2,1,0:T(8,128)(2,1)} pad(bf16[4,96,2,16,512]{4,3,2,1,0:T(8,128)(2,1)} %all-gather.3.cloned.1.call-done, bf16[]{:T(256)} %constant.129.clone.1), padding=0_0x6_0x0_0x0_0x0_0 | pad | bytes 25952258 | tf_op jit(solution)/shard_map/concatenate | solution.py:34
  100.5 64.7 %all-gather.5.cloned.1.call-done = bf16[4,96,2,16,512]{4,3,2,1,0:T(8,128)(2,1)} async-done(((bf16[4,6,2,16,512]{4,3,2,1,0:T(8,128)(2,1)}), bf16[4,96,2,16,512]{4,3,2,1,0:T(8,128)(2,1)}) %all-gather.5.cloned.1.call-update) | async-done | bytes 12582928 | tf_op jit(solution)/shard_map/all_gather | solution.py:39
  165.2 209.3 %while.20 = (s32[]{:T(128)}, f32[6,2,16,512]{3,2,1,0:T(8,128)S(1)}, f32[6,2,16,512]{3,2,1,0:T(8,128)S(1)}, f32[6,2,16,512]{3,2,1,0:T(8,128)S(1)}, f32[6,2,16,512...) while((s32[]{:T(128)}, f32[6,2,16,512]{3,2,1,0:T(8,128)S(1)}, ...), condition=%wide.region_1.2_spmd.clone, body=%wide.region_0.1_spmd.clone.sunk | while | flops 6684718 | bytes 7471932 | solution.py:62
  174.6 1.9 fusion.28
  176.5 1.8 fusion.29
  187.8 1.8 fusion.28
  189.5 1.8 fusion.29
  200.8 1.8 fusion.28
  202.6 1.8 fusion.29
  213.9 1.8 fusion.28
  215.7 1.8 fusion.29
  228.8 1.8 fusion.29
  241.9 1.8 fusion.29
  254.9 1.8 fusion.29
  268.1 1.8 fusion.29
  281.1 1.8 fusion.29
  294.2 1.8 fusion.29
  307.3 1.8 fusion.29
  320.4 1.8 fusion.29
  333.5 1.8 fusion.29
  346.5 1.8 fusion.29
  359.6 1.8 fusion.29
  372.7 1.8 fusion.29
  (144 shorter events, 97.6 us)
Async XLA Ops:
  6.5 59.3 %copy-start = (s32[16,16,3]{1,0,2:T(8,128)S(1)}, s32[16,16,3]{1,0,2:T(8,128)}, u32[]{:S(2)}) copy-start(s32[16,16,3]{1,0,2:T(8,128)} %param.10) | copy-start | bytes 9220
  6.5 82.6 %all-gather.3.cloned.1.call-start = ((), (), s32[]{:S(2)}) async-start(), calls=%async_computation | async-start | bytes 13369344 | tf_op jit(solution)/shard_map/all_gather | solution.py:32
  7.3 157.9 %all-gather.5.cloned.1.call-start = ((), (), s32[]{:S(2)}) async-start(), calls=%async_computation.1 | async-start | bytes 13369344 | tf_op jit(solution)/shard_map/all_gather | solution.py:39
  14.2 13.1 %collective-permute-start.9 = (bf16[4,6,2,1,1,512]{5,3,2,1,0,4:T(2,128)(2,1)S(1)}, bf16[4,6,2,1,1,512]{5,3,2,1,0,4:T(2,128)(2,1)S(1)}, u32[]{:S(2)}, u32[]{:S(2)}) collective-permute-start(bf16[4,6,2,1,1,512]{5,3,2,1,0,4:T(2,128)(2,1)S(1)} %get-tuple-element.260), channel_id=1, source_target_pairs={{0,10},{1,11},{2,8},{3,9},{4,14},{5,15},{6,12},{7,13},{8,2},{9,3},... | collective-permute-start | bytes 147464 | tf_op jit(solution)/shard_map/ppermute | solution.py:29
  20.5 7.3 %collective-permute-start.8 = (bf16[4,6,2,1,1,512]{5,3,2,1,0,4:T(2,128)(2,1)S(1)}, bf16[4,6,2,1,1,512]{5,3,2,1,0,4:T(2,128)(2,1)S(1)}, u32[]{:S(2)}, u32[]{:S(2)}) collective-permute-start(bf16[4,6,2,1,1,512]{5,3,2,1,0,4:T(2,128)(2,1)S(1)} %get-tuple-element.261), channel_id=1, source_target_pairs={{0,9},{1,8},{2,11},{3,10},{4,13},{5,12},{6,15},{7,14},{8,1},{9,0},... | collective-permute-start | bytes 147464 | tf_op jit(solution)/shard_map/ppermute | solution.py:29
  20.6 15.5 %collective-permute-start.7 = (bf16[4,6,2,1,1,512]{5,3,2,1,0,4:T(2,128)(2,1)S(1)}, bf16[4,6,2,1,1,512]{5,3,2,1,0,4:T(2,128)(2,1)S(1)}, u32[]{:S(2)}, u32[]{:S(2)}) collective-permute-start(bf16[4,6,2,1,1,512]{5,3,2,1,0,4:T(2,128)(2,1)S(1)} %get-tuple-element.262), channel_id=1, source_target_pairs={{0,8},{1,9},{2,10},{3,11},{4,12},{5,13},{6,14},{7,15},{8,0},{9,1},... | collective-permute-start | bytes 147464 | tf_op jit(solution)/shard_map/ppermute | solution.py:29
  23.5 12.9 %collective-permute-start.6 = (bf16[4,6,2,1,1,512]{5,3,2,1,0,4:T(2,128)(2,1)S(1)}, bf16[4,6,2,1,1,512]{5,3,2,1,0,4:T(2,128)(2,1)S(1)}, u32[]{:S(2)}, u32[]{:S(2)}) collective-permute-start(bf16[4,6,2,1,1,512]{5,3,2,1,0,4:T(2,128)(2,1)S(1)} %get-tuple-element.263), channel_id=1, source_target_pairs={{0,7},{1,6},{2,5},{3,4},{4,3},{5,2},{6,1},{7,0},{8,15},{9,14},{10,... | collective-permute-start | bytes 147464 | tf_op jit(solution)/shard_map/ppermute | solution.py:29
  23.8 14.0 %collective-permute-start.5 = (bf16[4,6,2,1,1,512]{5,3,2,1,0,4:T(2,128)(2,1)S(1)}, bf16[4,6,2,1,1,512]{5,3,2,1,0,4:T(2,128)(2,1)S(1)}, u32[]{:S(2)}, u32[]{:S(2)}) collective-permute-start(bf16[4,6,2,1,1,512]{5,3,2,1,0,4:T(2,128)(2,1)S(1)} %get-tuple-element.264), channel_id=1, source_target_pairs={{0,6},{1,7},{2,4},{3,5},{4,2},{5,3},{6,0},{7,1},{8,14},{9,15},{10,... | collective-permute-start | bytes 147464 | tf_op jit(solution)/shard_map/ppermute | solution.py:29
  27.4 12.0 %collective-permute-start.4 = (bf16[4,6,2,1,1,512]{5,3,2,1,0,4:T(2,128)(2,1)S(1)}, bf16[4,6,2,1,1,512]{5,3,2,1,0,4:T(2,128)(2,1)S(1)}, u32[]{:S(2)}, u32[]{:S(2)}) collective-permute-start(bf16[4,6,2,1,1,512]{5,3,2,1,0,4:T(2,128)(2,1)S(1)} %get-tuple-element.265), channel_id=1, source_target_pairs={{0,5},{1,4},{2,7},{3,6},{4,1},{5,0},{6,3},{7,2},{8,13},{9,12},{10,... | collective-permute-start | bytes 147464 | tf_op jit(solution)/shard_map/ppermute | solution.py:29
  27.8 14.7 %collective-permute-start.3 = (bf16[4,6,2,1,1,512]{5,3,2,1,0,4:T(2,128)(2,1)S(1)}, bf16[4,6,2,1,1,512]{5,3,2,1,0,4:T(2,128)(2,1)S(1)}, u32[]{:S(2)}, u32[]{:S(2)}) collective-permute-start(bf16[4,6,2,1,1,512]{5,3,2,1,0,4:T(2,128)(2,1)S(1)} %get-tuple-element.266), channel_id=1, source_target_pairs={{0,4},{1,5},{2,6},{3,7},{4,0},{5,1},{6,2},{7,3},{8,12},{9,13},{10,... | collective-permute-start | bytes 147464 | tf_op jit(solution)/shard_map/ppermute | solution.py:29
  36.1 7.4 %collective-permute-start.2 = (bf16[4,6,2,1,1,512]{5,3,2,1,0,4:T(2,128)(2,1)S(1)}, bf16[4,6,2,1,1,512]{5,3,2,1,0,4:T(2,128)(2,1)S(1)}, u32[]{:S(2)}, u32[]{:S(2)}) collective-permute-start(bf16[4,6,2,1,1,512]{5,3,2,1,0,4:T(2,128)(2,1)S(1)} %get-tuple-element.267), channel_id=1, source_target_pairs={{0,3},{1,2},{2,1},{3,0},{4,7},{5,6},{6,5},{7,4},{8,11},{9,10},{10,... | collective-permute-start | bytes 147464 | tf_op jit(solution)/shard_map/ppermute | solution.py:29
  36.5 8.7 %collective-permute-start.1 = (bf16[4,6,2,1,1,512]{5,3,2,1,0,4:T(2,128)(2,1)S(1)}, bf16[4,6,2,1,1,512]{5,3,2,1,0,4:T(2,128)(2,1)S(1)}, u32[]{:S(2)}, u32[]{:S(2)}) collective-permute-start(bf16[4,6,2,1,1,512]{5,3,2,1,0,4:T(2,128)(2,1)S(1)} %get-tuple-element.268), channel_id=1, source_target_pairs={{0,2},{1,3},{2,0},{3,1},{4,6},{5,7},{6,4},{7,5},{8,10},{9,11},{10,... | collective-permute-start | bytes 147464 | tf_op jit(solution)/shard_map/ppermute | solution.py:29
  37.8 9.8 %collective-permute-start = (bf16[4,6,2,1,1,512]{5,3,2,1,0,4:T(2,128)(2,1)S(1)}, bf16[4,6,2,1,1,512]{5,3,2,1,0,4:T(2,128)(2,1)S(1)}, u32[]{:S(2)}, u32[]{:S(2)}) collective-permute-start(bf16[4,6,2,1,1,512]{5,3,2,1,0,4:T(2,128)(2,1)S(1)} %get-tuple-element.269), channel_id=1, source_target_pairs={{0,1},{1,0},{2,3},{3,2},{4,5},{5,4},{6,7},{7,6},{8,9},{9,8},{10,11... | collective-permute-start | bytes 147464 | tf_op jit(solution)/shard_map/ppermute | solution.py:29
  39.4 21.1 %collective-permute-start.10 = (bf16[4,6,2,1,1,512]{5,3,2,1,0,4:T(2,128)(2,1)S(1)}, bf16[4,6,2,1,1,512]{5,3,2,1,0,4:T(2,128)(2,1)S(1)}, u32[]{:S(2)}, u32[]{:S(2)}) collective-permute-start(bf16[4,6,2,1,1,512]{5,3,2,1,0,4:T(2,128)(2,1)S(1)} %get-tuple-element.259), channel_id=1, source_target_pairs={{0,11},{1,10},{2,9},{3,8},{4,15},{5,14},{6,13},{7,12},{8,3},{9,2},... | collective-permute-start | bytes 147464 | tf_op jit(solution)/shard_map/ppermute | solution.py:29
  42.4 18.9 %collective-permute-start.11 = (bf16[4,6,2,1,1,512]{5,3,2,1,0,4:T(2,128)(2,1)S(1)}, bf16[4,6,2,1,1,512]{5,3,2,1,0,4:T(2,128)(2,1)S(1)}, u32[]{:S(2)}, u32[]{:S(2)}) collective-permute-start(bf16[4,6,2,1,1,512]{5,3,2,1,0,4:T(2,128)(2,1)S(1)} %get-tuple-element.258), channel_id=1, source_target_pairs={{0,12},{1,13},{2,14},{3,15},{4,8},{5,9},{6,10},{7,11},{8,4},{9,5},... | collective-permute-start | bytes 147464 | tf_op jit(solution)/shard_map/ppermute | solution.py:29
  43.6 18.7 %collective-permute-start.12 = (bf16[4,6,2,1,1,512]{5,3,2,1,0,4:T(2,128)(2,1)S(1)}, bf16[4,6,2,1,1,512]{5,3,2,1,0,4:T(2,128)(2,1)S(1)}, u32[]{:S(2)}, u32[]{:S(2)}) collective-permute-start(bf16[4,6,2,1,1,512]{5,3,2,1,0,4:T(2,128)(2,1)S(1)} %get-tuple-element.257), channel_id=1, source_target_pairs={{0,13},{1,12},{2,15},{3,14},{4,9},{5,8},{6,11},{7,10},{8,5},{9,4},... | collective-permute-start | bytes 147464 | tf_op jit(solution)/shard_map/ppermute | solution.py:29
  45.1 18.0 %collective-permute-start.13 = (bf16[4,6,2,1,1,512]{5,3,2,1,0,4:T(2,128)(2,1)S(1)}, bf16[4,6,2,1,1,512]{5,3,2,1,0,4:T(2,128)(2,1)S(1)}, u32[]{:S(2)}, u32[]{:S(2)}) collective-permute-start(bf16[4,6,2,1,1,512]{5,3,2,1,0,4:T(2,128)(2,1)S(1)} %get-tuple-element.256), channel_id=1, source_target_pairs={{0,14},{1,15},{2,12},{3,13},{4,10},{5,11},{6,8},{7,9},{8,6},{9,7},... | collective-permute-start | bytes 147464 | tf_op jit(solution)/shard_map/ppermute | solution.py:29
  47.6 16.4 %collective-permute-start.14 = (bf16[4,6,2,1,1,512]{5,3,2,1,0,4:T(2,128)(2,1)S(1)}, bf16[4,6,2,1,1,512]{5,3,2,1,0,4:T(2,128)(2,1)S(1)}, u32[]{:S(2)}, u32[]{:S(2)}) collective-permute-start(bf16[4,6,2,1,1,512]{5,3,2,1,0,4:T(2,128)(2,1)S(1)} %get-tuple-element.255), channel_id=1, source_target_pairs={{0,15},{1,14},{2,13},{3,12},{4,11},{5,10},{6,9},{7,8},{8,7},{9,6},... | collective-permute-start | bytes 147464 | tf_op jit(solution)/shard_map/ppermute | solution.py:29
  64.8 0.9 copy-start.1
Sparse Core Ops, SparseCore 0:
  9.2 79.8 all-gather.2
  91.0 74.1 all-gather.4
